TPU v7x, 32 devices: a whole 2x2x4 slice. The times are simulated.
32 devices in a mesh: req: 2 (over y), ctx: 16 (over z, x, core).
Axes of the slice: x: 2, y: 2, z: 4, core: 2. Of those that a mesh axis runs over, the one named last changes fastest.
Arguments:
- q_latent: bfloat16 [128, 48, 512], P(None, 'req'), parts along dimension 1, may hold values from -64 to 64
- q_rope: bfloat16 [128, 3072], P(None, 'req'), parts along dimension 1, may hold values from -6 to 6
- cache_latent: bfloat16 [128, 128, 512], P(('req', 'ctx')), parts along dimension 0, may hold values from -6 to 6
- cache_rope: bfloat16 [128, 64, 128], P(('req', 'ctx')), parts along dimension 0, may hold values from -6 to 6
- new_latent: bfloat16 [48, 512], P('req'), parts along dimension 0, may hold values from -6 to 6
- new_rope: bfloat16 [48, 64], P('req'), parts along dimension 0, may hold values from -6 to 6
- removed: int32 [24, 2], P('req'), parts along dimension 0, may hold values from 1 to 63, as said below
Outputs:
- attended: bfloat16 [128, 48, 512], P('ctx', 'req'), parts along dimension 1
There are 2 independent parts, one for each index of `req`. A program takes and returns all parts, laid end to end along the dimension named above; each array names one. Nothing has to cross between parts.
Inputs may be any that keep to these rules, and one draw needn't show every extreme that they name: Each row (first, last) names the blocks first to last - 1 of one removed span of whole blocks. Rows ascend, the spans are disjoint and are parted by at least one kept block; the first span starts at block 1 and the last ends at block 63.
All inputs are finite; a program needn't handle non-finite values.
Results may differ from a plain program's by a relative error of at most 0.0024.
Values may be sent and summed in bfloat16 or wider, within the bound.
No kernel may reach another device: no remote copies, remote signals or barrier semaphores. Data moves between devices by JAX's collectives and lax.ppermute only.
A program may use at most 64 MiB of HBM per device.

v0:
```python
import jax
import jax.numpy as jnp
import numpy as np
from jax import lax
from jax.sharding import PartitionSpec as P

floor_value = -1e30
score_scale = 192.0 ** (-0.5)


def rope_tables(rope_width):
    halves = rope_width // 2
    frequencies = 10000.0 ** (-2.0 * np.arange(halves) / rope_width)
    coarse = np.mod(4096.0 * frequencies, 2.0 * np.pi)
    middle = np.mod(64.0 * frequencies, 2.0 * np.pi)
    return (
        jnp.asarray(frequencies, jnp.float32),
        jnp.asarray(coarse, jnp.float32),
        jnp.asarray(middle, jnp.float32),
    )


def turn_angles(shift_rows, rope_width):
    frequencies, coarse, middle = rope_tables(rope_width)
    magnitude = jnp.abs(shift_rows)
    signed = jnp.where(shift_rows < 0, -1.0, 1.0).astype(jnp.float32)
    upper_part = (magnitude // 4096).astype(jnp.float32)[..., None]
    centre_part = (magnitude // 64 % 64).astype(jnp.float32)[..., None]
    lowest_part = (magnitude % 64).astype(jnp.float32)[..., None]
    angles = upper_part * coarse + centre_part * middle + lowest_part * frequencies
    return (jnp.cos(angles), signed[..., None] * jnp.sin(angles))


def rotate_last(values, cosine, sine_part):
    halves = values.shape[-1] // 2
    first_half = values[..., :halves]
    second_half = values[..., halves:]
    return jnp.concatenate(
        [
            first_half * cosine - second_half * sine_part,
            first_half * sine_part + second_half * cosine,
        ],
        axis=-1,
    )


def rotate_middle(values, cosine, sine_part):
    halves = values.shape[1] // 2
    first_half = values[:, :halves, :]
    second_half = values[:, halves:, :]
    return jnp.concatenate(
        [
            first_half * cosine - second_half * sine_part,
            first_half * sine_part + second_half * cosine,
        ],
        axis=1,
    )


def span_info(removed, total_blocks, block_rows):
    starts = removed[:, 0]
    finishes = removed[:, 1]
    block_ids = jnp.arange(total_blocks, dtype=jnp.int32)
    inside = (block_ids[:, None] >= starts[None, :]) & (block_ids[:, None] < finishes[None, :])
    kept_block = jnp.logical_not(jnp.any(inside, axis=1))
    drop_before = block_rows * jnp.sum(
        jnp.clip(block_ids[:, None], starts[None, :], finishes[None, :]) - starts[None, :], axis=1
    )
    kept_rows = total_blocks * block_rows - block_rows * jnp.sum(finishes - starts)
    return (kept_block, drop_before, kept_rows)


def block_terms(query_rows, rope_rows, latent_block, key_block):
    contract = (((1,), (1,)), ((), ()))
    scores = (
        lax.dot_general(query_rows, latent_block, contract, preferred_element_type=jnp.float32)
        + jnp.dot(rope_rows, key_block, preferred_element_type=jnp.float32)
    ) * score_scale
    block_max = jnp.max(scores, axis=1)
    weights = jnp.exp(scores - block_max[:, None]).astype(jnp.bfloat16)
    block_sum = jnp.sum(weights.astype(jnp.float32), axis=1)
    block_out = jnp.dot(weights, latent_block, preferred_element_type=jnp.float32)
    return (block_max, block_sum, block_out)


def absorb(carried, produced, kept_flag):
    run_max, run_sum, run_acc = carried
    block_max, block_sum, block_out = produced
    keep_part = kept_flag.astype(jnp.float32)
    lifted = jnp.where(kept_flag, block_max, floor_value)
    new_max = jnp.maximum(run_max, lifted)
    old_scale = jnp.exp(run_max - new_max)
    add_scale = jnp.exp(lifted - new_max) * keep_part
    return (
        new_max,
        run_sum * old_scale + block_sum * add_scale,
        run_acc * old_scale[:, None] + block_out * add_scale[:, None],
    )


def empty_state(row_total, lat_width):
    return (
        jnp.full((row_total,), floor_value, jnp.float32),
        jnp.zeros((row_total,), jnp.float32),
        jnp.zeros((row_total, lat_width), jnp.float32),
    )


def finish(own_max, own_sum, own_acc, own_rows, own_rope, new_latent, new_keys, tokens):
    row_total = own_rows.shape[0]
    own_max = own_max.reshape(row_total)
    own_sum = own_sum.reshape(row_total)
    own_acc = own_acc.reshape(row_total, new_latent.shape[1])
    contract = (((1,), (1,)), ((), ()))
    new_scores = (
        lax.dot_general(own_rows, new_latent, contract, preferred_element_type=jnp.float32)
        + lax.dot_general(own_rope, new_keys, contract, preferred_element_type=jnp.float32)
    ) * score_scale
    row_token = jnp.arange(row_total, dtype=jnp.int32) % tokens
    causal = jnp.arange(tokens, dtype=jnp.int32)[None, :] <= row_token[:, None]
    masked = jnp.where(causal, new_scores, floor_value)
    new_max = jnp.max(masked, axis=1)
    new_weights = jnp.where(causal, jnp.exp(masked - new_max[:, None]), 0.0).astype(jnp.bfloat16)
    new_sum = jnp.sum(new_weights.astype(jnp.float32), axis=1)
    new_out = jnp.dot(new_weights, new_latent, preferred_element_type=jnp.float32)
    top_score = jnp.maximum(own_max, new_max)
    old_part = jnp.exp(own_max - top_score)
    new_part = jnp.exp(new_max - top_score)
    numerator = own_acc * old_part[:, None] + new_out * new_part[:, None]
    denominator = own_sum * old_part + new_sum * new_part
    return (numerator / denominator[:, None]).astype(jnp.bfloat16)


def shards(q_latent, q_rope, cache_latent, cache_rope, new_latent, new_rope, removed):
    devices = lax.axis_size("ctx")
    my_index = lax.axis_index("ctx")
    local_blocks, block_rows, lat_width = cache_latent.shape
    head_count, tokens = (q_latent.shape[0], q_latent.shape[1])
    rope_width = new_rope.shape[1]
    own_heads = head_count // devices
    own_count = own_heads * tokens
    total_blocks = local_blocks * devices
    kept_block, drop_before, kept_rows = span_info(removed, total_blocks, block_rows)
    first_block = my_index * local_blocks
    kept_mine = lax.dynamic_slice_in_dim(kept_block, first_block, local_blocks)
    drop_mine = lax.dynamic_slice_in_dim(drop_before, first_block, local_blocks)
    cosine, sine_part = turn_angles(-drop_mine, rope_width)
    cache_keys = rotate_middle(
        cache_rope.astype(jnp.float32), cosine[:, :, None], sine_part[:, :, None]
    ).astype(jnp.bfloat16)
    positions = kept_rows + jnp.arange(tokens, dtype=jnp.int32)
    query_cos, query_sin = turn_angles(positions, rope_width)
    queries_rope = rotate_last(
        q_rope.reshape(head_count, tokens, rope_width).astype(jnp.float32), query_cos, query_sin
    )
    queries_rope = queries_rope.astype(jnp.bfloat16).reshape(head_count * tokens, rope_width)
    new_keys = rotate_last(new_rope.astype(jnp.float32), query_cos, query_sin).astype(jnp.bfloat16)
    query_rows = q_latent.reshape(head_count * tokens, lat_width)
    own_start = my_index * own_count
    own_rows = lax.dynamic_slice_in_dim(query_rows, own_start, own_count, 0)
    own_rope = lax.dynamic_slice_in_dim(queries_rope, own_start, own_count, 0)
    order_slots = jnp.argsort(jnp.logical_not(kept_mine).astype(jnp.int32), stable=True)
    slot_latent = jnp.take(cache_latent, order_slots, axis=0)
    slot_keys = jnp.take(cache_keys, order_slots, axis=0)
    filled = jnp.sum(kept_mine.astype(jnp.int32))

    def kept_step(index_slot, carried):
        latent_block = lax.dynamic_index_in_dim(slot_latent, index_slot, 0, keepdims=False)
        key_block = lax.dynamic_index_in_dim(slot_keys, index_slot, 0, keepdims=False)
        produced = block_terms(query_rows, queries_rope, latent_block, key_block)
        return absorb(carried, produced, jnp.asarray(True))

    run_max, run_sum, run_acc = lax.fori_loop(
        0, filled, kept_step, empty_state(head_count * tokens, lat_width)
    )
    maxima = run_max.reshape(head_count, tokens)
    top_score = lax.pmax(maxima, "ctx")
    factor = jnp.exp(maxima - top_score)
    own_acc, own_sum = (
        lax.psum_scatter(
            run_acc.reshape(head_count, tokens, lat_width) * factor[:, :, None],
            "ctx",
            scatter_dimension=0,
            tiled=True,
        ),
        lax.psum_scatter(
            run_sum.reshape(head_count, tokens) * factor, "ctx", scatter_dimension=0, tiled=True
        ),
    )
    own_max = lax.dynamic_slice_in_dim(top_score, my_index * own_heads, own_heads, 0)
    attended = finish(own_max, own_sum, own_acc, own_rows, own_rope, new_latent, new_keys, tokens)
    return attended.reshape(own_heads, tokens, lat_width)


def solution(mesh):
    in_specs = (
        P(None, "req", None),
        P(None, "req"),
        P(("req", "ctx"), None, None),
        P(("req", "ctx"), None, None),
        P("req", None),
        P("req", None),
        P("req", None),
    )
    out_specs = P("ctx", "req", None)
    return jax.shard_map(shards, mesh=mesh, in_specs=in_specs, out_specs=out_specs, check_vma=False)
```

profile of v0, /device:TPU:0, one launch (start us, length us, event | category | flops | bytes accessed | tf_op | source)
XLA Modules:
  0.0 216.7 jit_solution(2239655744903763529)
XLA Ops:
  6.6 1.4 subtract_reduce_fusion.1
  12.1 0.8 convert_element_type.67
  13.0 1.2 copy.23
  14.3 0.8 fusion.25
  17.5 1.8 concatenate.19
  19.8 1.8 concatenate.18
  22.0 3.5 %broadcast_in_dim.57 = f32[3072,512]{1,0:T(8,128)} broadcast(f32[]{:T(128)} %constant.150.clone.1), dimensions={} | broadcast | bytes 6291460 | tf_op jit(solution)/shard_map/broadcast_in_dim | solution.py:105
  25.5 28.7 %while.14 = (s32[]{:T(128)}, f32[3072]{0:T(1024)S(1)}, f32[3072]{0:T(1024)S(1)}, f32[3072,512]{1,0:T(8,128)}, s32[]{:T(128)}, /*index=5*/bf16[4,128,512]{2,1,0:T...) while((s32[]{:T(128)}, f32[3072]{0:T(1024)S(1)}, ...), condition=%wide.region_8.9_spmd, body=%wide.region_5.8_spmd.sunk | while | flops 863907840 | bytes 75161824 | solution.py:173
  26.2 3.2 %fusion.59 = f32[128,3072]{1,0:T(8,128)S(1)} fusion(bf16[3072,512]{1,0:T(8,128)(2,1)} %get-tuple-element.235, bf16[4,128,512]{2,1,0:T(8,128)(2,1)S(1)} %get-tuple-element.234, s32[]{:T(128)S(6)} %select_n.176), kind=kOutput, calls=%fused_computation.8.clone.1 | convolution fusion | flops 402653184 | bytes 4849668 | tf_op jit(solution)/shard_map/while/body/dot_general | solution.py:76
  30.1 2.1 multiply_add_fusion.8
  32.2 2.6 %copy-done.2 = f32[3072,512]{1,0:T(8,128)} copy-done((f32[3072,512]{1,0:T(8,128)}, f32[3072,512]{1,0:T(8,128)S(1)}, u32[]{:S(2)}) %copy-start.2) | copy-done | bytes 6291480 | tf_op jit(solution)/shard_map/while
  35.5 3.2 %fusion.59 = f32[128,3072]{1,0:T(8,128)S(1)} fusion(bf16[3072,512]{1,0:T(8,128)(2,1)} %get-tuple-element.235, bf16[4,128,512]{2,1,0:T(8,128)(2,1)S(1)} %get-tuple-element.234, s32[]{:T(128)S(6)} %select_n.176), kind=kOutput, calls=%fused_computation.8.clone.1 | convolution fusion | flops 402653184 | bytes 4849668 | tf_op jit(solution)/shard_map/while/body/dot_general | solution.py:76
  39.4 2.1 multiply_add_fusion.8
  41.5 2.6 %copy-done.2 = f32[3072,512]{1,0:T(8,128)} copy-done((f32[3072,512]{1,0:T(8,128)}, f32[3072,512]{1,0:T(8,128)S(1)}, u32[]{:S(2)}) %copy-start.2) | copy-done | bytes 6291480 | tf_op jit(solution)/shard_map/while
  44.9 3.2 %fusion.59 = f32[128,3072]{1,0:T(8,128)S(1)} fusion(bf16[3072,512]{1,0:T(8,128)(2,1)} %get-tuple-element.235, bf16[4,128,512]{2,1,0:T(8,128)(2,1)S(1)} %get-tuple-element.234, s32[]{:T(128)S(6)} %select_n.176), kind=kOutput, calls=%fused_computation.8.clone.1 | convolution fusion | flops 402653184 | bytes 4849668 | tf_op jit(solution)/shard_map/while/body/dot_general | solution.py:76
  48.8 2.1 multiply_add_fusion.8
  50.8 2.6 %copy-done.2 = f32[3072,512]{1,0:T(8,128)} copy-done((f32[3072,512]{1,0:T(8,128)}, f32[3072,512]{1,0:T(8,128)S(1)}, u32[]{:S(2)}) %copy-start.2) | copy-done | bytes 6291480 | tf_op jit(solution)/shard_map/while
  54.3 57.7 %pmax.7 = f32[128,24]{1,0:T(8,128)S(1)} all-reduce(f32[128,24]{1,0:T(8,128)S(1)} %reshape.496), channel_id=1, replica_groups=mesh['req'=2,'ctx'=16] {'ctx'}, use_global_device_ids=true, to_apply=%region_9.10 | all-reduce | flops 3072 | bytes 24576 | tf_op jit(solution)/shard_map/pmax | solution.py:177
  112.1 6.0 %broadcast_multiply_fusion = f32[128,24,512]{2,1,0:T(8,128)} fusion(f32[128,24,512]{2,1,0:T(8,128)} %bitcast.44, f32[128,24]{1,0:T(8,128)S(1)} %get-tuple-element.113), kind=kLoop, calls=%fused_computation.20 | loop fusion | flops 1572864 | bytes 12595200 | tf_op jit(solution)/shard_map/mul | solution.py:181
  119.9 59.0 %all-reduce = f32[128,24]{1,0:T(8,128)S(1)} all-reduce(f32[128,24]{1,0:T(8,128)S(1)} %get-tuple-element.112), channel_id=3, replica_groups=mesh['req'=2,'ctx'=16] {'ctx'}, use_global_device_ids=true, to_apply=%region_12.13.clone | all-reduce | flops 3072 | bytes 24576
  179.0 1.1 fusion.16
  180.4 27.5 %reduce-scatter.2.cloned.1.call-done = f32[8,24,512]{2,1,0:T(8,128)} async-done(((f32[128,24,512]{2,1,0:T(8,128)}), f32[8,24,512]{2,1,0:T(8,128)}) %reduce-scatter.2.cloned.1.call-update) | async-done | bytes 393232 | tf_op jit(solution)/shard_map/reduce_scatter | solution.py:180
  207.8 1.1 bitcast_multiply_fusion
  208.9 0.9 fusion.13
  (79 shorter events, 10.6 us)
Async XLA Ops:
  6.5 9.2 %copy-start = (bf16[4,128,512]{2,1,0:T(8,128)(2,1)S(1)}, bf16[4,128,512]{2,1,0:T(8,128)(2,1)}, u32[]{:S(2)}) copy-start(bf16[4,128,512]{2,1,0:T(8,128)(2,1)} %param.17) | copy-start | bytes 1572868
  6.5 10.0 %copy-start.4 = (f32[32]{0:T(128)S(1)}, f32[32]{0:T(128)}, u32[]{:S(2)}) copy-start(f32[32]{0:T(128)} %constant.175.clone) | copy-start | bytes 388
  6.5 10.0 %copy-start.5 = (f32[32]{0:T(128)S(1)}, f32[32]{0:T(128)}, u32[]{:S(2)}) copy-start(f32[32]{0:T(128)} %constant.174.clone) | copy-start | bytes 388
  6.5 10.0 %copy-start.6 = (f32[32]{0:T(128)S(1)}, f32[32]{0:T(128)}, u32[]{:S(2)}) copy-start(f32[32]{0:T(128)} %constant.173.clone) | copy-start | bytes 388
  6.5 201.3 %reduce-scatter.2.cloned.1.call-start = ((), (), s32[]{:S(2)}) async-start(), calls=%async_computation.1 | async-start | bytes 6684672 | tf_op jit(solution)/shard_map/reduce_scatter | solution.py:180
  26.2 3.9 %copy-start.1 = (f32[3072,512]{1,0:T(8,128)S(1)}, f32[3072,512]{1,0:T(8,128)}, u32[]{:S(2)}) copy-start(f32[3072,512]{1,0:T(8,128)} %get-tuple-element.220) | copy-start | bytes 18874372 | tf_op jit(solution)/shard_map/while
  32.2 2.7 %copy-start.2 = (f32[3072,512]{1,0:T(8,128)}, f32[3072,512]{1,0:T(8,128)S(1)}, u32[]{:S(2)}) copy-start(f32[3072,512]{1,0:T(8,128)S(1)} %multiply_add_fusion.8) | copy-start | bytes 18874372 | tf_op jit(solution)/shard_map/while
  35.5 3.9 %copy-start.1 = (f32[3072,512]{1,0:T(8,128)S(1)}, f32[3072,512]{1,0:T(8,128)}, u32[]{:S(2)}) copy-start(f32[3072,512]{1,0:T(8,128)} %get-tuple-element.220) | copy-start | bytes 18874372 | tf_op jit(solution)/shard_map/while
  41.5 2.7 %copy-start.2 = (f32[3072,512]{1,0:T(8,128)}, f32[3072,512]{1,0:T(8,128)S(1)}, u32[]{:S(2)}) copy-start(f32[3072,512]{1,0:T(8,128)S(1)} %multiply_add_fusion.8) | copy-start | bytes 18874372 | tf_op jit(solution)/shard_map/while
  44.9 3.9 %copy-start.1 = (f32[3072,512]{1,0:T(8,128)S(1)}, f32[3072,512]{1,0:T(8,128)}, u32[]{:S(2)}) copy-start(f32[3072,512]{1,0:T(8,128)} %get-tuple-element.220) | copy-start | bytes 18874372 | tf_op jit(solution)/shard_map/while
  50.8 2.7 %copy-start.2 = (f32[3072,512]{1,0:T(8,128)}, f32[3072,512]{1,0:T(8,128)S(1)}, u32[]{:S(2)}) copy-start(f32[3072,512]{1,0:T(8,128)S(1)} %multiply_add_fusion.8) | copy-start | bytes 18874372 | tf_op jit(solution)/shard_map/while
  118.0 0.7 copy-start.7
  118.0 60.9 %copy-start.3 = (bf16[24,512]{1,0:T(8,128)(2,1)S(1)}, bf16[24,512]{1,0:T(8,128)(2,1)}, u32[]{:S(2)}) copy-start(bf16[24,512]{1,0:T(8,128)(2,1)} %param.19) | copy-start | bytes 73732
Sparse Core Ops, SparseCore 0:
  118.2 89.5 reduce-scatter.1
where the time goes:
time: 219 us; the launch traced here: 217 us
  blocking collectives  117 us (53%)
  waiting for transfers between devices  27.5 us (13%)
  local copies, waits for them, and re-layouts  21 us (10%)
  matrix products  19.3 us (9%)
  between operations  15 us (7%)
  other arithmetic  14.4 us (7%)
  loops' own time  3 us (1%)
    unnamed x1, blocking collectives  59 us
    pmax x1, blocking collectives, shards(): top_score = lax.pmax(maxima, 'ctx')  57.7 us
    reduce_scatter x1, waiting for transfers between devices, shards(): lax.psum_scatter(run_acc.reshape(head_count, tokens, lat_width) * factor[...  27.5 us
    dot_general x3, matrix products, block_terms(): lax.dot_general(query_rows, latent_block, contract, preferred_element_typ...  9.54 us
    while x12, local copies, waits for them, and re-layouts  7.96 us
    dot_general x3, matrix products, block_terms(): jnp.dot(weights, latent_block, preferred_element_type=jnp.float32)  6.2 us
    mul x1, other arithmetic, shards(): run_acc.reshape(head_count, tokens, lat_width) * factor[:, :, None]  5.96 us
  transfers between devices with their start and end apart: 1, of which 1 were waited for; matrix products, arithmetic and copies ran while one was open for 1% of the time, Pallas kernels for 0%

commit v1 on v0

v1 whole, which is shorter than its diff:
```python
import functools

import jax
import jax.numpy as jnp
import numpy as np
from jax import lax
from jax.experimental import pallas as pl
from jax.experimental.pallas import tpu as pltpu
from jax.sharding import PartitionSpec as P

floor_value = -1e30
score_scale = 192.0 ** (-0.5)
code_top = 32767.0
contract_last = (((1,), (1,)), ((), ()))
contract_first = (((0,), (0,)), ((), ()))


def rope_tables(rope_width):
    halves = rope_width // 2
    frequencies = 10000.0 ** (-2.0 * np.arange(halves) / rope_width)
    coarse = np.mod(4096.0 * frequencies, 2.0 * np.pi)
    middle = np.mod(64.0 * frequencies, 2.0 * np.pi)
    return (
        jnp.asarray(frequencies, jnp.float32),
        jnp.asarray(coarse, jnp.float32),
        jnp.asarray(middle, jnp.float32),
    )


def turn_angles(shift_rows, rope_width, axis):
    spread = (lambda v: v[:, None]) if axis == 0 else (lambda v: v[None, :])
    across = (lambda v: v[None, :]) if axis == 0 else (lambda v: v[:, None])
    frequencies, coarse, middle = (spread(t) for t in rope_tables(rope_width))
    magnitude = jnp.abs(shift_rows)
    signed = across(jnp.where(shift_rows < 0, -1.0, 1.0).astype(jnp.float32))
    upper_part = across((magnitude // 4096).astype(jnp.float32))
    centre_part = across((magnitude // 64 % 64).astype(jnp.float32))
    lowest_part = across((magnitude % 64).astype(jnp.float32))
    angles = upper_part * coarse + centre_part * middle + lowest_part * frequencies
    return (jnp.cos(angles), signed * jnp.sin(angles))


def rotate_last(values, cosine, sine_part):
    halves = values.shape[-1] // 2
    first_half = values[..., :halves]
    second_half = values[..., halves:]
    return jnp.concatenate(
        [
            first_half * cosine - second_half * sine_part,
            first_half * sine_part + second_half * cosine,
        ],
        axis=-1,
    )


def fill_blocks(lat_refs, rope_refs, cos_ref, sin_ref, turned_ref, keys_ref):
    position = 0
    for lat_ref, rope_ref in zip(lat_refs, rope_refs):
        count, width, _ = rope_ref.shape
        halves = width // 2
        for b in range(count):
            cosine = cos_ref[:, position : position + 1]
            sine_part = sin_ref[:, position : position + 1]
            upper = rope_ref[b, :halves, :].astype(jnp.float32)
            lower = rope_ref[b, halves:, :].astype(jnp.float32)
            keys = jnp.concatenate(
                [upper * cosine - lower * sine_part, upper * sine_part + lower * cosine], axis=0
            )
            keys_ref[position] = keys.T.astype(jnp.bfloat16)
            turned_ref[position] = lat_ref[b].T
            position += 1


def stack(refs, ids):
    parts = [refs[i][0] for i in ids]
    return parts[0] if len(parts) == 1 else jnp.concatenate(parts, axis=0)


def absorb(query, rope, kept, lat_refs, turned_ref, keys_ref, run_max, run_sum, old_acc):
    blocks = [ref[b] for ref in lat_refs for b in range(ref.shape[0])]
    lifted, flags, sums, weights = [], [], [], []
    for b, latent in enumerate(blocks):
        scores = (
            lax.dot_general(latent, query, contract_last, preferred_element_type=jnp.float32)
            + lax.dot_general(keys_ref[b], rope, contract_last, preferred_element_type=jnp.float32)
        ) * score_scale
        block_max = jnp.max(scores, axis=0, keepdims=True)
        weight = jnp.exp(scores - block_max).astype(jnp.bfloat16)
        sums.append(jnp.sum(weight.astype(jnp.float32), axis=0, keepdims=True))
        weights.append(weight)
        flags.append(kept[b] != 0)
        lifted.append(jnp.where(flags[-1], block_max, floor_value))
    new_max = functools.reduce(jnp.maximum, lifted, run_max)
    old_scale = jnp.exp(run_max - new_max)
    factors = [jnp.where(f, jnp.exp(m - new_max), 0.0) for f, m in zip(flags, lifted)]
    new_sum = run_sum * old_scale
    for s, f in zip(sums, factors):
        new_sum = new_sum + s * f
    width = turned_ref.shape[1]
    chunk = min(128, width)
    acc = []
    for c in range(0, width, chunk):
        total = None if old_acc is None else old_acc(c, chunk) * old_scale
        for b, weight in enumerate(weights):
            term = jnp.dot(turned_ref[b, c : c + chunk, :], weight, preferred_element_type=jnp.float32) * factors[b]
            total = term if total is None else total + term
        acc.append(total)
    return new_max, new_sum, acc


def pack_stats(*rows):
    lanes = rows[0].shape[1]
    return jnp.concatenate([*rows, jnp.zeros((8 - len(rows), lanes), jnp.float32)], axis=0)


def encode(acc):
    reach = functools.reduce(jnp.maximum, [jnp.max(jnp.abs(a), axis=0, keepdims=True) for a in acc])
    reach = jnp.maximum(reach, 1e-30)
    gain = code_top / reach
    codes = [jnp.round(a * gain).astype(jnp.int32).astype(jnp.int16) for a in acc]
    return codes, reach * (1.0 / code_top)


def decode(codes):
    return codes.astype(jnp.int32).astype(jnp.float32)


def write_coded(acc, new_max, new_sum, code_refs, stat_refs, ids, lanes):
    codes, scale = encode(acc)
    stats = pack_stats(new_max, new_sum, scale)
    chunk = codes[0].shape[0]
    for n, i in enumerate(ids):
        span = slice(n * lanes, (n + 1) * lanes)
        stat_refs[i][...] = stats[:, span]
        for c, part in enumerate(codes):
            code_refs[i][c * chunk : (c + 1) * chunk, :] = part[:, span]


def tiles_of(count, lanes, most=256):
    step = max(1, most // lanes)
    return [list(range(i, min(i + step, count))) for i in range(0, count, step)]


def queries(refs, rope_ref, ids, lanes):
    span = slice(ids[0] * lanes, (ids[-1] + 1) * lanes)
    query = stack(refs, ids) if len(refs) > 1 else refs[0][0, span, :]
    return query, rope_ref[span, :]


def early_kernel(plan, dest, kept, *refs):
    slots, lanes, parts, per, n_q = plan
    q_refs, refs = refs[:n_q], refs[n_q:]
    rope_ref, cos_ref, sin_ref, refs = *refs[:3], refs[3:]
    lat_refs, rope_refs, refs = refs[:parts], refs[parts : 2 * parts], refs[2 * parts :]
    sends = slots // per
    code_refs, stat_refs = refs[:sends], refs[sends : 2 * sends]
    turned_ref, keys_ref = refs[2 * sends :]
    fill_blocks(lat_refs, rope_refs, cos_ref, sin_ref, turned_ref, keys_ref)
    for ids in tiles_of(slots, lanes):
        query, rope = queries(q_refs, rope_ref, ids, lanes)
        run_max = jnp.full((1, query.shape[0]), floor_value, jnp.float32)
        new_max, new_sum, acc = absorb(
            query, rope, kept, lat_refs, turned_ref, keys_ref, run_max, jnp.zeros_like(run_max), None
        )
        write_coded(
            acc, new_max, new_sum, code_refs, stat_refs, range(ids[0] // per, (ids[-1] + 1) // per), lanes * per
        )


def near_kernel(plan, dest, kept, *refs):
    slots, lanes, parts, tokens, n_q = plan
    q_refs, refs = refs[:n_q], refs[n_q:]
    rope_ref, cos_ref, sin_ref, own_q, own_rope, new_lat, new_keys, refs = *refs[:7], refs[7:]
    lat_refs, rope_refs, refs = refs[:parts], refs[parts : 2 * parts], refs[2 * parts :]
    stat_out, acc_out, new_stat, new_out, turned_ref, keys_ref = refs
    fill_blocks(lat_refs, rope_refs, cos_ref, sin_ref, turned_ref, keys_ref)
    for ids in tiles_of(slots, lanes):
        query, rope = queries(q_refs, rope_ref, ids, lanes)
        span = slice(ids[0] * lanes, (ids[-1] + 1) * lanes)
        run_max = jnp.full((1, query.shape[0]), floor_value, jnp.float32)
        new_max, new_sum, acc = absorb(
            query, rope, kept, lat_refs, turned_ref, keys_ref, run_max, jnp.zeros_like(run_max), None
        )
        stat_out[:, span] = pack_stats(new_max, new_sum)
        chunk = acc[0].shape[0]
        for c, part in enumerate(acc):
            acc_out[c * chunk : (c + 1) * chunk, span] = part
    latent = new_lat[...]
    scores = (
        lax.dot_general(latent, own_q[0], contract_last, preferred_element_type=jnp.float32)
        + lax.dot_general(new_keys[...], own_rope[...], contract_last, preferred_element_type=jnp.float32)
    ) * score_scale
    row_token = lax.broadcasted_iota(jnp.int32, scores.shape, 1) % tokens
    causal = lax.broadcasted_iota(jnp.int32, scores.shape, 0) <= row_token
    masked = jnp.where(causal, scores, floor_value)
    top = jnp.max(masked, axis=0, keepdims=True)
    weights = jnp.where(causal, jnp.exp(masked - top), 0.0).astype(jnp.bfloat16)
    new_stat[...] = pack_stats(top, jnp.sum(weights.astype(jnp.float32), axis=0, keepdims=True))
    new_out[...] = lax.dot_general(latent, weights, contract_first, preferred_element_type=jnp.float32)


def far_kernel(plan, dest, kept, *refs):
    slots, lanes, parts, n_q = plan
    q_refs, refs = refs[:n_q], refs[n_q:]
    rope_ref, cos_ref, sin_ref, stat_in, acc_in, refs = *refs[:5], refs[5:]
    lat_refs, rope_refs, refs = refs[:parts], refs[parts : 2 * parts], refs[2 * parts :]
    code_refs, stat_refs = refs[:slots], refs[slots : 2 * slots]
    turned_ref, keys_ref = refs[2 * slots :]
    fill_blocks(lat_refs, rope_refs, cos_ref, sin_ref, turned_ref, keys_ref)
    for ids in tiles_of(slots, lanes):
        query, rope = queries(q_refs, rope_ref, ids, lanes)
        span = slice(ids[0] * lanes, (ids[-1] + 1) * lanes)
        new_max, new_sum, acc = absorb(
            query,
            rope,
            kept,
            lat_refs,
            turned_ref,
            keys_ref,
            stat_in[0:1, span],
            stat_in[1:2, span],
            lambda c, size, span=span: acc_in[c : c + size, span],
        )
        write_coded(acc, new_max, new_sum, code_refs, stat_refs, ids, lanes)


def join(stats, values, first=None):
    top = functools.reduce(jnp.maximum, [s[0] for s in stats])
    factors = [jnp.exp(s[0] - top) for s in stats]
    total = functools.reduce(jnp.add, [f * s[1] for f, s in zip(factors, stats)])
    return top, factors, total


def middle_kernel(plan, *refs):
    lanes, per, count = plan
    code_refs, stat_refs, refs = refs[:count], refs[count : 2 * count], refs[2 * count :]
    own_out, own_stat, refs = refs[0], refs[1], refs[2:]
    sent, sent_stats = refs[: per - 1], refs[per - 1 :]
    stats = [r[...] for r in stat_refs]
    top, factors, total = join([(s[0:1], s[1:2]) for s in stats], None)
    gains = [f * s[2:3] for f, s in zip(factors, stats)]
    width = own_out.shape[0]
    chunk = min(128, width)
    acc = []
    for c in range(0, width, chunk):
        terms = [decode(r[c : c + chunk, :]) * g for r, g in zip(code_refs, gains)]
        acc.append(functools.reduce(jnp.add, terms))
    for c, part in enumerate(acc):
        own_out[c * chunk : (c + 1) * chunk, :] = part[:, :lanes]
    own_stat[...] = pack_stats(top, total)[:, :lanes]
    codes, scale = encode(acc)
    stats = pack_stats(top, total, scale)
    for n in range(per - 1):
        span = slice((n + 1) * lanes, (n + 2) * lanes)
        sent_stats[n][...] = stats[:, span]
        for c, part in enumerate(codes):
            sent[n][c * chunk : (c + 1) * chunk, :] = part[:, span]


def last_kernel(plan, *refs):
    lanes_a, lanes_b, groups, per = plan
    new_stat, new_out, refs = refs[0], refs[1], refs[2:]
    codes_a, stats_a, refs = refs[:groups], refs[groups : 2 * groups], refs[2 * groups :]
    result = refs[-1]
    sections = [(slice(0, lanes_a), [], codes_a, stats_a)]
    if lanes_b:
        own_b, own_stat, refs = refs[0], refs[1], refs[2:]
        sections.append((slice(lanes_a, lanes_a + lanes_b), [(own_b, own_stat)], refs[: per - 1], refs[per - 1 : -1]))
    width = new_out.shape[0]
    chunk = min(128, width)
    prepared = []
    for span, plain, codes, coded_stats in sections:
        stats = [new_stat[:, span]] + [s[...] for _, s in plain] + [s[...] for s in coded_stats]
        _, factors, total = join([(s[0:1], s[1:2]) for s in stats], None)
        known = 1 + len(plain)
        gains = factors[:known] + [f * s[2:3] for f, s in zip(factors[known:], stats[known:])]
        prepared.append((gains, total))
    for c in range(0, width, chunk):
        piece = slice(c, c + chunk)
        columns = []
        for (span, plain, codes, _), (gains, total) in zip(sections, prepared):
            values = [new_out[piece, span]] + [v[piece, :] for v, _ in plain] + [decode(v[piece, :]) for v in codes]
            numerator = functools.reduce(jnp.add, [v * g for v, g in zip(values, gains)])
            columns.append(numerator / total)
        merged = columns[0] if len(columns) == 1 else jnp.concatenate(columns, axis=1)
        result[:, piece] = merged.T.astype(jnp.bfloat16)


def whole(shape):
    return pl.BlockSpec(tuple(shape), lambda *_: (0,) * len(shape))


def gather_size(devices):
    size = 1
    while (2 * size) ** 2 <= devices and devices % (2 * size) == 0:
        size *= 2
    return size


def shards(q_latent, q_rope, cache_latent, cache_rope, new_latent, new_rope, removed):
    devices = lax.axis_size("ctx")
    me = lax.axis_index("ctx")
    blocks, block_rows, lat_width = cache_latent.shape
    head_count, tokens = (q_latent.shape[0], q_latent.shape[1])
    rope_width = new_rope.shape[1]
    own_heads = head_count // devices
    rows = own_heads * tokens
    size = gather_size(devices)
    pair = min(2, size)
    per = size // pair
    groups = devices // size
    lanes_b = rows // 3 if rows % 192 == 0 and per > 1 else 0
    lanes_a = rows - lanes_b

    def swap(value, k):
        return lax.ppermute(value, "ctx", [(i, i ^ k) for i in range(devices)])

    latents, ropes = {0: cache_latent}, {0: cache_rope}
    if size > 1:
        latents[1], ropes[1] = swap(cache_latent, 1), swap(cache_rope, 1)
    for k in range(2, size, 2):
        latents[k], ropes[k] = swap(cache_latent, k), swap(cache_rope, k)
    for k in range(2, size, 2):
        latents[k + 1], ropes[k + 1] = swap(latents[k], 1), swap(ropes[k], 1)

    starts, finishes = removed[:, 0][:, None], removed[:, 1][:, None]
    members = me ^ jnp.arange(size, dtype=jnp.int32)
    block_ids = (members[:, None] * blocks + jnp.arange(blocks, dtype=jnp.int32)[None, :]).reshape(1, -1)
    inside = (block_ids >= starts) & (block_ids < finishes)
    kept = jnp.logical_not(jnp.any(inside, axis=0)).astype(jnp.int32)
    drop = block_rows * jnp.sum(jnp.clip(block_ids, starts, finishes) - starts, axis=0)
    kept_rows = blocks * devices * block_rows - block_rows * jnp.sum(finishes - starts)
    cosine, sine_part = turn_angles(-drop, rope_width, 0)
    positions = kept_rows + jnp.arange(tokens, dtype=jnp.int32)
    query_cos, query_sin = turn_angles(positions, rope_width, 1)
    new_keys = rotate_last(new_rope.astype(jnp.float32), query_cos, query_sin).astype(jnp.bfloat16)

    along_z = size * jnp.arange(groups, dtype=jnp.int32)
    along_x = pair * jnp.arange(per, dtype=jnp.int32)
    dest = (me ^ along_z[:, None] ^ along_x[None, :]).reshape(-1)
    dest_a = me ^ along_z
    slabs = q_latent.reshape(devices, rows, lat_width)
    packed = q_rope.reshape(devices, own_heads, tokens * rope_width)
    turn = dest if lanes_b else dest_a
    rope_slabs = jnp.take(packed, turn, axis=0).reshape(turn.shape[0], own_heads, tokens, rope_width)
    rope_slabs = rotate_last(rope_slabs.astype(jnp.float32), query_cos, query_sin)
    rope_slabs = rope_slabs.astype(jnp.bfloat16).reshape(groups, -1, rows, rope_width)
    rope_a = rope_slabs[:, 0, :lanes_a].reshape(groups * lanes_a, rope_width)
    own_rope = rope_slabs[0, 0]

    def call(kernel, scalars, ins, specs, outs, scratch=(), flops=10**7):
        return pl.pallas_call(
            kernel,
            grid_spec=pltpu.PrefetchScalarGridSpec(
                num_scalar_prefetch=len(scalars),
                grid=(1,),
                in_specs=specs,
                out_specs=[whole(o.shape) for o in outs],
                scratch_shapes=list(scratch),
            ),
            out_shape=outs,
            cost_estimate=pl.CostEstimate(flops=flops, bytes_accessed=10**6, transcendentals=0),
        )(*scalars, *ins)

    def query_rows(ids, count, first):
        number = ids.shape[0]
        if count % 16 == 0 and first % count == 0:
            at = first // count
            return [slabs] * number, [
                pl.BlockSpec((1, count, lat_width), lambda t, d, *_, i=i: (d[i], at, 0)) for i in range(number)
            ]
        chosen = jnp.take(slabs, ids, axis=0)[:, first : first + count].reshape(1, number * count, lat_width)
        return [chosen], [whole(chosen.shape)]

    def cache_of(members):
        span = slice(members[0] * blocks, (members[-1] + 1) * blocks)
        arrays = [latents[k] for k in members] + [ropes[k] for k in members]
        scratch = [
            pltpu.VMEM((len(members) * blocks, lat_width, block_rows), jnp.bfloat16),
            pltpu.VMEM((len(members) * blocks, block_rows, rope_width), jnp.bfloat16),
        ]
        return span, [cosine[:, span], sine_part[:, span]], arrays, scratch

    def shape(dtype, *dims):
        return jax.ShapeDtypeStruct(dims, dtype)

    near, far = list(range(pair)), list(range(pair, size))
    span, tables, arrays, scratch = cache_of(near)
    extras = [*tables]
    if lanes_b:
        rope_b = rope_slabs[:, :, lanes_a:].reshape(groups * per * lanes_b, rope_width)
        q_in, q_specs = query_rows(dest, lanes_b, lanes_a)
        ins = [rope_b, *tables, *arrays]
        out = call(
            functools.partial(early_kernel, (groups * per, lanes_b, pair, per, len(q_in))),
            [dest, kept[span]],
            [*q_in, *ins],
            [*q_specs, *[whole(v.shape) for v in ins]],
            [shape(jnp.int16, lat_width, per * lanes_b)] * groups + [shape(jnp.float32, 8, per * lanes_b)] * groups,
            scratch,
            10**9,
        )
        codes_b, stats_b = list(out[:groups]), list(out[groups:])
        for k in range(1, groups):
            codes_b[k], stats_b[k] = swap(codes_b[k], k * size), swap(stats_b[k], k * size)
    qa_in, qa_specs = query_rows(dest_a, lanes_a, 0)
    ins = [rope_a, *tables, slabs, own_rope, new_latent, new_keys, *arrays]
    specs = [whole(v.shape) for v in ins]
    specs[3] = pl.BlockSpec((1, rows, lat_width), lambda t, d, *_: (d[0], 0, 0))
    near_stat, near_acc, new_stat, new_out = call(
        functools.partial(near_kernel, (groups, lanes_a, pair, tokens, len(qa_in))),
        [dest_a, kept[span]],
        [*qa_in, *ins],
        [*qa_specs, *specs],
        [
            shape(jnp.float32, 8, groups * lanes_a),
            shape(jnp.float32, lat_width, groups * lanes_a),
            shape(jnp.float32, 8, rows),
            shape(jnp.float32, lat_width, rows),
        ],
        scratch,
        10**9,
    )
    span, tables, arrays, scratch = cache_of(far)
    ins = [rope_a, *tables, near_stat, near_acc, *arrays]
    out = call(
        functools.partial(far_kernel, (groups, lanes_a, len(far), len(qa_in))),
        [dest_a, kept[span]],
        [*qa_in, *ins],
        [*qa_specs, *[whole(v.shape) for v in ins]],
        [shape(jnp.int16, lat_width, lanes_a)] * groups + [shape(jnp.float32, 8, lanes_a)] * groups,
        scratch,
        10**9,
    )
    codes_a, stats_a = list(out[:groups]), list(out[groups:])
    for k in range(1, groups):
        codes_a[k], stats_a[k] = swap(codes_a[k], k * size), swap(stats_a[k], k * size)
    ins = [new_stat, new_out, *codes_a, *stats_a]
    if lanes_b:
        given = [*codes_b, *stats_b]
        out = call(
            functools.partial(middle_kernel, (lanes_b, per, groups)),
            [],
            given,
            [whole(v.shape) for v in given],
            [shape(jnp.float32, lat_width, lanes_b), shape(jnp.float32, 8, lanes_b)]
            + [shape(jnp.int16, lat_width, lanes_b)] * (per - 1)
            + [shape(jnp.float32, 8, lanes_b)] * (per - 1),
        )
        own_b, own_stat, sent, sent_stats = out[0], out[1], list(out[2 : 1 + per]), list(out[1 + per :])
        for n in range(per - 1):
            sent[n], sent_stats[n] = swap(sent[n], (n + 1) * pair), swap(sent_stats[n], (n + 1) * pair)
        ins = [*ins, own_b, own_stat, *sent, *sent_stats]
    (attended,) = call(
        functools.partial(last_kernel, (lanes_a, lanes_b, groups, per)),
        [],
        ins,
        [whole(v.shape) for v in ins],
        [shape(jnp.bfloat16, rows, lat_width)],
    )
    return attended.reshape(own_heads, tokens, lat_width)


def solution(mesh):
    in_specs = (
        P(None, "req", None),
        P(None, "req"),
        P(("req", "ctx"), None, None),
        P(("req", "ctx"), None, None),
        P("req", None),
        P("req", None),
        P("req", None),
    )
    out_specs = P("ctx", "req", None)
    return jax.shard_map(shards, mesh=mesh, in_specs=in_specs, out_specs=out_specs, check_vma=False)
```

time: 219 us -> 72.5 us (0.33)
  blocking collectives: 117 us -> 0 us
  Pallas kernels: 0 us -> 24.3 us
  starting transfers between devices: 0.03 us -> 23.3 us
  matrix products: 19.3 us -> 0 us
  local copies, waits for them, and re-layouts: 21 us -> 4.59 us
  waiting for transfers between devices: 27.5 us -> 12.1 us
  between operations: 15 us -> 1.01 us
  other arithmetic: 14.4 us -> 6.86 us
  loops' own time: 3 us -> 0 us
    unnamed x1 -> x0, blocking collectives: 59 us -> none
    pmax x1 -> x0, blocking collectives: 57.7 us -> none  [shards(): top_score = lax.pmax(maxima, 'ctx')]
    reduce_scatter x1 -> x0, waiting for transfers between devices: 27.5 us -> none  [shards(): lax.psum_scatter(run_acc.reshape(head_count, tokens, lat_width) * factor[...]
    pallas_call x0 -> x5, Pallas kernels: none -> 24.3 us  [call(): pl.pallas_call(kernel, grid_spec=pltpu.PrefetchScalarGridSpec(num_scalar_...]
    ppermute x0 -> x20, starting transfers between devices: none -> 23.3 us  [swap(): return lax.ppermute(value, 'ctx', [(i, i ^ k) for i in range(devices)])]
    dot_general x12 -> x0, matrix products: 19.3 us -> none  [the longest x3 9.54 us: block_terms(): lax.dot_general(query_rows, latent_block, contract, preferred_element_typ...]
    ppermute x0 -> x20, waiting for transfers between devices: none -> 12.1 us  [swap(): return lax.ppermute(value, 'ctx', [(i, i ^ k) for i in range(devices)])]
    while x13 -> x0, local copies, waits for them, and re-layouts: 8.33 us -> none
  transfers between devices with their start and end apart: 1 -> 20, of which waited for: 1 -> 5; matrix products, arithmetic and copies ran while one was open for 1% -> 13% of each run, Pallas kernels for 0% -> 30%
where the time goes in v1:
time: 72.5 us; the launch traced here: 72.2 us
  Pallas kernels  24.3 us (34%)
  starting transfers between devices  23.3 us (32%)
  waiting for transfers between devices  12.1 us (17%)
  other arithmetic  6.86 us (9%)
  local copies, waits for them, and re-layouts  4.59 us (6%)
  between operations  1.01 us (1%)
    pallas_call x5, Pallas kernels, call(): pl.pallas_call(kernel, grid_spec=pltpu.PrefetchScalarGridSpec(num_scalar_...  24.3 us
    ppermute x20, starting transfers between devices, swap(): return lax.ppermute(value, 'ctx', [(i, i ^ k) for i in range(devices)])  23.3 us
    ppermute x20, waiting for transfers between devices, swap(): return lax.ppermute(value, 'ctx', [(i, i ^ k) for i in range(devices)])  12.1 us
    unnamed x58, local copies, waits for them, and re-layouts  2.23 us
    concatenate x3, other arithmetic, rotate_last(): jnp.concatenate([first_half * cosine - second_half * sine_part, first_hal...  2.19 us
  transfers between devices with their start and end apart: 20, of which 5 were waited for; matrix products, arithmetic and copies ran while one was open for 13% of the time, Pallas kernels for 30%

profile of v1, /device:TPU:0, one launch (start us, length us, event | category | flops | bytes accessed | tf_op | source)
XLA Modules:
  0.0 72.2 jit_solution(7959127227015876102)
XLA Ops:
  0.5 2.5 %collective-permute-start.2 = (bf16[4,128,512]{2,1,0:T(8,128)(2,1)}, bf16[4,128,512]{2,1,0:T(8,128)(2,1)S(1)}, u32[]{:S(2)}, u32[]{:S(2)}) collective-permute-start(bf16[4,128,512]{2,1,0:T(8,128)(2,1)} %refs_11_.3), channel_id=1, source_target_pairs={{0,2},{1,3},{2,0},{3,1},{4,6},{5,7},{6,4},{7,5},{8,10},{9,11},{10,... | collective-permute-start | bytes 1572872 | tf_op jit(solution)/shard_map/ppermute | solution.py:316
  3.5 1.4 %subtract_reduce_fusion.1 = (s32[]{:T(128)}, s32[12]{0:T(128)S(1)}, s32[12]{0:T(128)S(1)}) fusion(s32[12,2]{0,1:T(2,128)} %param.19), kind=kLoop, calls=%fused_computation.64 | loop fusion | flops 23 | bytes 196 | tf_op jit(solution)/shard_map/reduce_sum | solution.py:332
  8.0 0.8 %subtract_convert_fusion.1 = (bf16[24,32]{1,0:T(8,128)(2,1)S(1)}, bf16[24,32]{1,0:T(8,128)(2,1)S(1)}, f32[24,32]{1,0:T(8,128)S(1)}, f32[24,32]{1,0:T(8,128)S(1)}) fusion(f32[24,64]{1,0:T(8,128)S(1)} %convert_element_type.62, f32[32]{0:T(128)} %constant.117.clone, f32[24]{0:T(128)S(1)} %get-tuple-element.74, f32[32]{0:T(128)} %constant.119.clone, ...), kind=kLoop, calls=%fused_computation.16 | loop fusion | flops 10752 | bytes 16128 | tf_op jit(solution)/shard_map/convert
  12.3 3.8 %collective-permute-done.2.refs_9_ = bf16[4,128,512]{2,1,0:T(8,128)(2,1)S(1)} collective-permute-done((bf16[4,128,512]{2,1,0:T(8,128)(2,1)}, bf16[4,128,512]{2,1,0:T(8,128)(2,1)S(1)}, u32[]{:S(2)}, u32[]{:S(2)}) %collective-permute-start.2) | collective-permute-done | bytes 524320 | tf_op jit(solution)/shard_map/ppermute | solution.py:316
  18.6 6.4 %shard_map.129 = (s16[512,128]{1,0:T(8,128)(2,1)}, s16[512,128]{1,0:T(8,128)(2,1)}, s16[512,128]{1,0:T(8,128)(2,1)}, s16[512,128]{1,0:T(8,128)(2,1)}, f32[8,128]...) custom-call(s32[8]{0:T(128)} %copy-done.22, s32[8]{0:T(128)} %get-tuple-element.69.kept, ...), custom_call_target="tpu_custom_call" | custom-call | flops 1000000000 | bytes 1000000 | tf_op jit(solution)/shard_map/pallas_call | solution.py:352
  25.0 2.2 %collective-permute-start.12 = (s16[512,128]{1,0:T(8,128)(2,1)}, s16[512,128]{1,0:T(8,128)(2,1)S(1)}, u32[]{:S(2)}, u32[]{:S(2)}) collective-permute-start(s16[512,128]{1,0:T(8,128)(2,1)} %get-tuple-element.42), channel_id=1, source_target_pairs={{0,4},{1,5},{2,6},{3,7},{4,0},{5,1},{6,2},{7,3},{8,12},{9,13},{10,... | collective-permute-start | bytes 393224 | tf_op jit(solution)/shard_map/ppermute | solution.py:316
  27.1 2.6 %collective-permute-start.13 = (s16[512,128]{1,0:T(8,128)(2,1)}, s16[512,128]{1,0:T(8,128)(2,1)S(1)}, u32[]{:S(2)}, u32[]{:S(2)}) collective-permute-start(s16[512,128]{1,0:T(8,128)(2,1)} %get-tuple-element.43), channel_id=1, source_target_pairs={{0,8},{1,9},{2,10},{3,11},{4,12},{5,13},{6,14},{7,15},{8,0},{9,1},... | collective-permute-start | bytes 393224 | tf_op jit(solution)/shard_map/ppermute | solution.py:316
  30.2 6.9 %shard_map.127 = (f32[8,512]{1,0:T(8,128)}, f32[512,512]{1,0:T(8,128)}, f32[8,192]{1,0:T(8,128)}, f32[512,192]{1,0:T(8,128)}) custom-call(s32[4]{0:T(128)} %copy-done.14, s32[8]{0:T(128)} %get-tuple-element.69.kept, bf16[16,192,512]{2,1,0:T(8,128)(2,1)} %bitcast.24, bf16[16,192,512]{2,1,0:T(8,128)(2,1)} %bitcast.25, bf16[16,192,512]{2,1,0:T(8,128)(2,1)} %bitcast.26, ...), custom_call_target="tpu_custom_call" | custom-call | flops 1000000000 | bytes 1000000 | tf_op jit(solution)/shard_map/pallas_call | solution.py:352
  37.1 1.4 %collective-permute-start.14 = (s16[512,128]{1,0:T(8,128)(2,1)S(1)}, s16[512,128]{1,0:T(8,128)(2,1)S(1)}, u32[]{:S(2)}, u32[]{:S(2)}) collective-permute-start(s16[512,128]{1,0:T(8,128)(2,1)S(1)} %copy-done.26), channel_id=1, source_target_pairs={{0,12},{1,13},{2,14},{3,15},{4,8},{5,9},{6,10},{7,11},{8,4},{9,5},... | collective-permute-start | bytes 393224 | tf_op jit(solution)/shard_map/ppermute | solution.py:316
  38.5 1.8 %collective-permute-start.16 = (f32[8,128]{1,0:T(8,128)S(1)}, f32[8,128]{1,0:T(8,128)S(1)}, u32[]{:S(2)}, u32[]{:S(2)}) collective-permute-start(f32[8,128]{1,0:T(8,128)S(1)} %copy-done.28), channel_id=1, source_target_pairs={{0,8},{1,9},{2,10},{3,11},{4,12},{5,13},{6,14},{7,15},{8,0},{9,1},... | collective-permute-start | bytes 12296 | tf_op jit(solution)/shard_map/ppermute | solution.py:316
  40.3 1.0 %collective-permute-start.17 = (f32[8,128]{1,0:T(8,128)S(1)}, f32[8,128]{1,0:T(8,128)S(1)}, u32[]{:S(2)}, u32[]{:S(2)}) collective-permute-start(f32[8,128]{1,0:T(8,128)S(1)} %copy-done.27), channel_id=1, source_target_pairs={{0,12},{1,13},{2,14},{3,15},{4,8},{5,9},{6,10},{7,11},{8,4},{9,5},... | collective-permute-start | bytes 12296 | tf_op jit(solution)/shard_map/ppermute | solution.py:316
  41.3 6.7 %shard_map.128 = (s16[512,128]{1,0:T(8,128)(2,1)}, s16[512,128]{1,0:T(8,128)(2,1)}, s16[512,128]{1,0:T(8,128)(2,1)}, s16[512,128]{1,0:T(8,128)(2,1)}, f32[8,128]...) custom-call(s32[4]{0:T(128)} %copy-done.14, s32[8]{0:T(128)} %get-tuple-element.68.kept, ...), custom_call_target="tpu_custom_call" | custom-call | flops 1000000000 | bytes 1000000 | tf_op jit(solution)/shard_map/pallas_call | solution.py:352
  48.0 1.2 %collective-permute-start.6 = (s16[512,128]{1,0:T(8,128)(2,1)}, s16[512,128]{1,0:T(8,128)(2,1)S(1)}, u32[]{:S(2)}, u32[]{:S(2)}) collective-permute-start(s16[512,128]{1,0:T(8,128)(2,1)} %get-tuple-element.34), channel_id=1, source_target_pairs={{0,4},{1,5},{2,6},{3,7},{4,0},{5,1},{6,2},{7,3},{8,12},{9,13},{10,... | collective-permute-start | bytes 393224 | tf_op jit(solution)/shard_map/ppermute | solution.py:316
  49.2 2.3 %collective-permute-start.7 = (s16[512,128]{1,0:T(8,128)(2,1)}, s16[512,128]{1,0:T(8,128)(2,1)S(1)}, u32[]{:S(2)}, u32[]{:S(2)}) collective-permute-start(s16[512,128]{1,0:T(8,128)(2,1)} %get-tuple-element.35), channel_id=1, source_target_pairs={{0,8},{1,9},{2,10},{3,11},{4,12},{5,13},{6,14},{7,15},{8,0},{9,1},... | collective-permute-start | bytes 393224 | tf_op jit(solution)/shard_map/ppermute | solution.py:316
  51.5 0.9 %collective-permute-start.8 = (s16[512,128]{1,0:T(8,128)(2,1)}, s16[512,128]{1,0:T(8,128)(2,1)S(1)}, u32[]{:S(2)}, u32[]{:S(2)}) collective-permute-start(s16[512,128]{1,0:T(8,128)(2,1)} %get-tuple-element.36), channel_id=1, source_target_pairs={{0,12},{1,13},{2,14},{3,15},{4,8},{5,9},{6,10},{7,11},{8,4},{9,5},... | collective-permute-start | bytes 393224 | tf_op jit(solution)/shard_map/ppermute | solution.py:316
  53.2 2.0 %shard_map.130 = (f32[512,64]{1,0:T(8,128)}, f32[8,64]{1,0:T(8,128)}, s16[512,64]{1,0:T(8,128)(2,1)}, f32[8,64]{1,0:T(8,128)}) custom-call(s16[512,128]{1,0:T(8,128)(2,1)} %get-tuple-element.41.refs_0_, s16[512,128]{1,0:T(8,128)(2,1)} %copy-done.9, s16[512,128]{1,0:T(8,128)(2,1)} %copy-done.10, s16[512,128]{1,0:T(8,128)(2,1)} %copy-done.11, ...), custom_call_target="tpu_custom_call" | custom-call | flops 10000000 | bytes 1000000 | tf_op jit(solution)/shard_map/pallas_call | solution.py:352
  55.3 1.5 %collective-permute-start.18 = (s16[512,64]{1,0:T(8,128)(2,1)}, s16[512,64]{1,0:T(8,128)(2,1)S(1)}, u32[]{:S(2)}, u32[]{:S(2)}) collective-permute-start(s16[512,64]{1,0:T(8,128)(2,1)} %get-tuple-element.51), channel_id=1, source_target_pairs={{0,2},{1,3},{2,0},{3,1},{4,6},{5,7},{6,4},{7,5},{8,10},{9,11},{10,... | collective-permute-start | bytes 196616 | tf_op jit(solution)/shard_map/ppermute | solution.py:316
  57.3 3.3 %collective-permute-done.19.refs_13_ = f32[8,64]{1,0:T(8,128)S(1)} collective-permute-done((f32[8,64]{1,0:T(8,128)}, f32[8,64]{1,0:T(8,128)S(1)}, u32[]{:S(2)}, u32[]{:S(2)}) %collective-permute-start.19) | collective-permute-done | bytes 2080 | tf_op jit(solution)/shard_map/ppermute | solution.py:316
  60.6 1.0 %collective-permute-start.10 = (f32[8,128]{1,0:T(8,128)}, f32[8,128]{1,0:T(8,128)S(1)}, u32[]{:S(2)}, u32[]{:S(2)}) collective-permute-start(f32[8,128]{1,0:T(8,128)} %get-tuple-element.39), channel_id=1, source_target_pairs={{0,8},{1,9},{2,10},{3,11},{4,12},{5,13},{6,14},{7,15},{8,0},{9,1},... | collective-permute-start | bytes 12296 | tf_op jit(solution)/shard_map/ppermute | solution.py:316
  61.5 2.0 %collective-permute-start.11 = (f32[8,128]{1,0:T(8,128)}, f32[8,128]{1,0:T(8,128)S(1)}, u32[]{:S(2)}, u32[]{:S(2)}) collective-permute-start(f32[8,128]{1,0:T(8,128)} %get-tuple-element.40), channel_id=1, source_target_pairs={{0,12},{1,13},{2,14},{3,15},{4,8},{5,9},{6,10},{7,11},{8,4},{9,5},... | collective-permute-start | bytes 12296 | tf_op jit(solution)/shard_map/ppermute | solution.py:316
  63.5 1.8 %collective-permute-done.10.refs_8_ = f32[8,128]{1,0:T(8,128)S(1)} collective-permute-done((f32[8,128]{1,0:T(8,128)}, f32[8,128]{1,0:T(8,128)S(1)}, u32[]{:S(2)}, u32[]{:S(2)}) %collective-permute-start.10) | collective-permute-done | bytes 4128 | tf_op jit(solution)/shard_map/ppermute | solution.py:316
  65.8 1.3 %collective-permute-done.11.refs_9_ = f32[8,128]{1,0:T(8,128)S(1)} collective-permute-done((f32[8,128]{1,0:T(8,128)}, f32[8,128]{1,0:T(8,128)S(1)}, u32[]{:S(2)}, u32[]{:S(2)}) %collective-permute-start.11) | collective-permute-done | bytes 4128 | tf_op jit(solution)/shard_map/ppermute | solution.py:316
  67.2 1.9 %collective-permute-done.9.refs_7_ = f32[8,128]{1,0:T(8,128)S(1)} collective-permute-done((f32[8,128]{1,0:T(8,128)}, f32[8,128]{1,0:T(8,128)S(1)}, u32[]{:S(2)}, u32[]{:S(2)}) %collective-permute-start.9) | collective-permute-done | bytes 4128 | tf_op jit(solution)/shard_map/ppermute | solution.py:316
  69.9 2.3 %shard_map.131 = bf16[192,512]{1,0:T(8,128)(2,1)} custom-call(f32[8,192]{1,0:T(8,128)} %get-tuple-element.29.refs_0_, f32[512,192]{1,0:T(8,128)} %get-tuple-element.30.refs_1_, s16[512,128]{1,0:T(8,128)(2,1)} %get-tuple-element.33.refs_2_, s16[512,128]{1,0:T(8,128)(2,1)} %copy-done.5, s16[512,128]{1,0:T(8,128)(2,1)} %copy-done.6, s16[512,128]{1,0:T(8,128)(2,1)} %copy-done.7, ...), custom_call_target="tpu_custom_call" | custom-call | flops 10000000 | bytes 1000000 | tf_op jit(solution)/shard_map/pallas_call | solution.py:352
  (112 shorter events, 12.2 us)
Async XLA Ops:
  0.0 17.8 %collective-permute-start = (bf16[4,128,512]{2,1,0:T(8,128)(2,1)}, bf16[4,128,512]{2,1,0:T(8,128)(2,1)S(1)}, u32[]{:S(2)}, u32[]{:S(2)}) collective-permute-start(bf16[4,128,512]{2,1,0:T(8,128)(2,1)} %refs_11_.3), channel_id=1, source_target_pairs={{0,1},{1,0},{2,3},{3,2},{4,5},{5,4},{6,7},{7,6},{8,9},{9,8},{10,11... | collective-permute-start | bytes 1572872 | tf_op jit(solution)/shard_map/ppermute | solution.py:316
  0.5 15.5 %collective-permute-start.2 = (bf16[4,128,512]{2,1,0:T(8,128)(2,1)}, bf16[4,128,512]{2,1,0:T(8,128)(2,1)S(1)}, u32[]{:S(2)}, u32[]{:S(2)}) collective-permute-start(bf16[4,128,512]{2,1,0:T(8,128)(2,1)} %refs_11_.3), channel_id=1, source_target_pairs={{0,2},{1,3},{2,0},{3,1},{4,6},{5,7},{6,4},{7,5},{8,10},{9,11},{10,... | collective-permute-start | bytes 1572872 | tf_op jit(solution)/shard_map/ppermute | solution.py:316
  3.0 14.7 %collective-permute-start.1 = (bf16[4,64,128]{2,1,0:T(8,128)(2,1)}, bf16[4,64,128]{2,1,0:T(8,128)(2,1)S(1)}, u32[]{:S(2)}, u32[]{:S(2)}) collective-permute-start(bf16[4,64,128]{2,1,0:T(8,128)(2,1)} %refs_13_.3), channel_id=1, source_target_pairs={{0,1},{1,0},{2,3},{3,2},{4,5},{5,4},{6,7},{7,6},{8,9},{9,8},{10,11... | collective-permute-start | bytes 196616 | tf_op jit(solution)/shard_map/ppermute | solution.py:316
  3.2 14.1 %collective-permute-start.4 = (bf16[4,64,128]{2,1,0:T(8,128)(2,1)}, bf16[4,64,128]{2,1,0:T(8,128)(2,1)S(1)}, u32[]{:S(2)}, u32[]{:S(2)}) collective-permute-start(bf16[4,64,128]{2,1,0:T(8,128)(2,1)} %refs_13_.3), channel_id=1, source_target_pairs={{0,2},{1,3},{2,0},{3,1},{4,6},{5,7},{6,4},{7,5},{8,10},{9,11},{10,... | collective-permute-start | bytes 196616 | tf_op jit(solution)/shard_map/ppermute | solution.py:316
  16.0 8.9 %copy-start.2 = (bf16[4,128,512]{2,1,0:T(8,128)(2,1)}, bf16[4,128,512]{2,1,0:T(8,128)(2,1)S(1)}, u32[]{:S(2)}) copy-start(bf16[4,128,512]{2,1,0:T(8,128)(2,1)S(1)} %collective-permute-done.2.refs_9_) | copy-start | bytes 1572868
  16.0 24.2 %collective-permute-start.3 = (bf16[4,128,512]{2,1,0:T(8,128)(2,1)S(1)}, bf16[4,128,512]{2,1,0:T(8,128)(2,1)S(1)}, u32[]{:S(2)}, u32[]{:S(2)}) collective-permute-start(bf16[4,128,512]{2,1,0:T(8,128)(2,1)S(1)} %collective-permute-done.2.refs_9_), channel_id=1, source_target_pairs={{0,1},{1,0},{2,3},{3,2},{4,5},{5,4},{6,7},{7,6},{8,9},{9,8},{10,11... | collective-permute-start | bytes 1572872 | tf_op jit(solution)/shard_map/ppermute | solution.py:316
  17.3 19.7 %collective-permute-start.5 = (bf16[4,64,128]{2,1,0:T(8,128)(2,1)S(1)}, bf16[4,64,128]{2,1,0:T(8,128)(2,1)S(1)}, u32[]{:S(2)}, u32[]{:S(2)}) collective-permute-start(bf16[4,64,128]{2,1,0:T(8,128)(2,1)S(1)} %collective-permute-done.4.refs_11_), channel_id=1, source_target_pairs={{0,1},{1,0},{2,3},{3,2},{4,5},{5,4},{6,7},{7,6},{8,9},{9,8},{10,11... | collective-permute-start | bytes 196616 | tf_op jit(solution)/shard_map/ppermute | solution.py:316
  25.0 26.6 %collective-permute-start.12 = (s16[512,128]{1,0:T(8,128)(2,1)}, s16[512,128]{1,0:T(8,128)(2,1)S(1)}, u32[]{:S(2)}, u32[]{:S(2)}) collective-permute-start(s16[512,128]{1,0:T(8,128)(2,1)} %get-tuple-element.42), channel_id=1, source_target_pairs={{0,4},{1,5},{2,6},{3,7},{4,0},{5,1},{6,2},{7,3},{8,12},{9,13},{10,... | collective-permute-start | bytes 393224 | tf_op jit(solution)/shard_map/ppermute | solution.py:316
  27.1 25.4 %collective-permute-start.13 = (s16[512,128]{1,0:T(8,128)(2,1)}, s16[512,128]{1,0:T(8,128)(2,1)S(1)}, u32[]{:S(2)}, u32[]{:S(2)}) collective-permute-start(s16[512,128]{1,0:T(8,128)(2,1)} %get-tuple-element.43), channel_id=1, source_target_pairs={{0,8},{1,9},{2,10},{3,11},{4,12},{5,13},{6,14},{7,15},{8,0},{9,1},... | collective-permute-start | bytes 393224 | tf_op jit(solution)/shard_map/ppermute | solution.py:316
  29.7 8.8 %collective-permute-start.15 = (f32[8,128]{1,0:T(8,128)}, f32[8,128]{1,0:T(8,128)S(1)}, u32[]{:S(2)}, u32[]{:S(2)}) collective-permute-start(f32[8,128]{1,0:T(8,128)} %get-tuple-element.46), channel_id=1, source_target_pairs={{0,4},{1,5},{2,6},{3,7},{4,0},{5,1},{6,2},{7,3},{8,12},{9,13},{10,... | collective-permute-start | bytes 12296 | tf_op jit(solution)/shard_map/ppermute | solution.py:316
  30.2 10.1 %copy-start.27 = (f32[8,128]{1,0:T(8,128)S(1)}, f32[8,128]{1,0:T(8,128)}, u32[]{:S(2)}) copy-start(f32[8,128]{1,0:T(8,128)} %get-tuple-element.48) | copy-start | bytes 12292
  37.1 15.4 %collective-permute-start.14 = (s16[512,128]{1,0:T(8,128)(2,1)S(1)}, s16[512,128]{1,0:T(8,128)(2,1)S(1)}, u32[]{:S(2)}, u32[]{:S(2)}) collective-permute-start(s16[512,128]{1,0:T(8,128)(2,1)S(1)} %copy-done.26), channel_id=1, source_target_pairs={{0,12},{1,13},{2,14},{3,15},{4,8},{5,9},{6,10},{7,11},{8,4},{9,5},... | collective-permute-start | bytes 393224 | tf_op jit(solution)/shard_map/ppermute | solution.py:316
  38.5 9.5 %copy-start.15 = (f32[8,128]{1,0:T(8,128)}, f32[8,128]{1,0:T(8,128)S(1)}, u32[]{:S(2)}) copy-start(f32[8,128]{1,0:T(8,128)S(1)} %collective-permute-done.15.refs_5_) | copy-start | bytes 12292
  38.5 9.5 %collective-permute-start.16 = (f32[8,128]{1,0:T(8,128)S(1)}, f32[8,128]{1,0:T(8,128)S(1)}, u32[]{:S(2)}, u32[]{:S(2)}) collective-permute-start(f32[8,128]{1,0:T(8,128)S(1)} %copy-done.28), channel_id=1, source_target_pairs={{0,8},{1,9},{2,10},{3,11},{4,12},{5,13},{6,14},{7,15},{8,0},{9,1},... | collective-permute-start | bytes 12296 | tf_op jit(solution)/shard_map/ppermute | solution.py:316
  40.3 8.9 %collective-permute-start.17 = (f32[8,128]{1,0:T(8,128)S(1)}, f32[8,128]{1,0:T(8,128)S(1)}, u32[]{:S(2)}, u32[]{:S(2)}) collective-permute-start(f32[8,128]{1,0:T(8,128)S(1)} %copy-done.27), channel_id=1, source_target_pairs={{0,12},{1,13},{2,14},{3,15},{4,8},{5,9},{6,10},{7,11},{8,4},{9,5},... | collective-permute-start | bytes 12296 | tf_op jit(solution)/shard_map/ppermute | solution.py:316
  48.0 21.1 %collective-permute-start.6 = (s16[512,128]{1,0:T(8,128)(2,1)}, s16[512,128]{1,0:T(8,128)(2,1)S(1)}, u32[]{:S(2)}, u32[]{:S(2)}) collective-permute-start(s16[512,128]{1,0:T(8,128)(2,1)} %get-tuple-element.34), channel_id=1, source_target_pairs={{0,4},{1,5},{2,6},{3,7},{4,0},{5,1},{6,2},{7,3},{8,12},{9,13},{10,... | collective-permute-start | bytes 393224 | tf_op jit(solution)/shard_map/ppermute | solution.py:316
  49.2 19.9 %collective-permute-start.7 = (s16[512,128]{1,0:T(8,128)(2,1)}, s16[512,128]{1,0:T(8,128)(2,1)S(1)}, u32[]{:S(2)}, u32[]{:S(2)}) collective-permute-start(s16[512,128]{1,0:T(8,128)(2,1)} %get-tuple-element.35), channel_id=1, source_target_pairs={{0,8},{1,9},{2,10},{3,11},{4,12},{5,13},{6,14},{7,15},{8,0},{9,1},... | collective-permute-start | bytes 393224 | tf_op jit(solution)/shard_map/ppermute | solution.py:316
  51.5 17.6 %collective-permute-start.8 = (s16[512,128]{1,0:T(8,128)(2,1)}, s16[512,128]{1,0:T(8,128)(2,1)S(1)}, u32[]{:S(2)}, u32[]{:S(2)}) collective-permute-start(s16[512,128]{1,0:T(8,128)(2,1)} %get-tuple-element.36), channel_id=1, source_target_pairs={{0,12},{1,13},{2,14},{3,15},{4,8},{5,9},{6,10},{7,11},{8,4},{9,5},... | collective-permute-start | bytes 393224 | tf_op jit(solution)/shard_map/ppermute | solution.py:316
  55.3 6.3 %collective-permute-start.18 = (s16[512,64]{1,0:T(8,128)(2,1)}, s16[512,64]{1,0:T(8,128)(2,1)S(1)}, u32[]{:S(2)}, u32[]{:S(2)}) collective-permute-start(s16[512,64]{1,0:T(8,128)(2,1)} %get-tuple-element.51), channel_id=1, source_target_pairs={{0,2},{1,3},{2,0},{3,1},{4,6},{5,7},{6,4},{7,5},{8,10},{9,11},{10,... | collective-permute-start | bytes 196616 | tf_op jit(solution)/shard_map/ppermute | solution.py:316
  56.7 3.8 %collective-permute-start.19 = (f32[8,64]{1,0:T(8,128)}, f32[8,64]{1,0:T(8,128)S(1)}, u32[]{:S(2)}, u32[]{:S(2)}) collective-permute-start(f32[8,64]{1,0:T(8,128)} %get-tuple-element.52), channel_id=1, source_target_pairs={{0,2},{1,3},{2,0},{3,1},{4,6},{5,7},{6,4},{7,5},{8,10},{9,11},{10,... | collective-permute-start | bytes 6152 | tf_op jit(solution)/shard_map/ppermute | solution.py:316
  60.6 8.6 %copy-start.18 = (f32[8,64]{1,0:T(8,128)}, f32[8,64]{1,0:T(8,128)S(1)}, u32[]{:S(2)}) copy-start(f32[8,64]{1,0:T(8,128)S(1)} %collective-permute-done.19.refs_13_) | copy-start | bytes 6148
  60.6 4.7 %collective-permute-start.10 = (f32[8,128]{1,0:T(8,128)}, f32[8,128]{1,0:T(8,128)S(1)}, u32[]{:S(2)}, u32[]{:S(2)}) collective-permute-start(f32[8,128]{1,0:T(8,128)} %get-tuple-element.39), channel_id=1, source_target_pairs={{0,8},{1,9},{2,10},{3,11},{4,12},{5,13},{6,14},{7,15},{8,0},{9,1},... | collective-permute-start | bytes 12296 | tf_op jit(solution)/shard_map/ppermute | solution.py:316
  61.5 5.6 %collective-permute-start.11 = (f32[8,128]{1,0:T(8,128)}, f32[8,128]{1,0:T(8,128)S(1)}, u32[]{:S(2)}, u32[]{:S(2)}) collective-permute-start(f32[8,128]{1,0:T(8,128)} %get-tuple-element.40), channel_id=1, source_target_pairs={{0,12},{1,13},{2,14},{3,15},{4,8},{5,9},{6,10},{7,11},{8,4},{9,5},... | collective-permute-start | bytes 12296 | tf_op jit(solution)/shard_map/ppermute | solution.py:316
  65.3 3.8 %collective-permute-start.9 = (f32[8,128]{1,0:T(8,128)}, f32[8,128]{1,0:T(8,128)S(1)}, u32[]{:S(2)}, u32[]{:S(2)}) collective-permute-start(f32[8,128]{1,0:T(8,128)} %get-tuple-element.38), channel_id=1, source_target_pairs={{0,4},{1,5},{2,6},{3,7},{4,0},{5,1},{6,2},{7,3},{8,12},{9,13},{10,... | collective-permute-start | bytes 12296 | tf_op jit(solution)/shard_map/ppermute | solution.py:316
  (25 other events, 83.8 us)
